TPU v7x, 256 devices: a whole 4x4x8 slice. The times are simulated.
256 devices in a mesh: ctx: 32 (over x_hi, z, core), tp: 8 (over x_lo, y).
Axes of the slice: x: 4 (x_hi: 2, x_lo: 2; x = x_hi * 2 + x_lo), y: 4, z: 8, core: 2. Of those that a mesh axis runs over, the one named last changes fastest.
Arguments:
- features: bfloat16 [3, 4096, 8192], P(None, 'ctx', 'tp'), may hold values from -6 to 6
- conv_weight: float32 [3, 3, 8192], replicated, may hold values from -3 to 3
- decay_rates: float32 [16, 8192], P(None, ('tp', 'ctx')), may hold values from 1e-05 to 0.03
- residues: float32 [16, 8192], P(None, ('tp', 'ctx')), may hold values from -1.5 to 1.5
- skip_gain: float32 [8192], P(('tp', 'ctx')), may hold values from -1 to 1
- out_weight: bfloat16 [8192, 8192], P('tp', 'ctx'), may hold values from -0.0625 to 0.0625
Outputs:
- mixed: bfloat16 [4096, 8192], P('ctx', 'tp')
All inputs are finite; a program needn't handle non-finite values.
Results may differ from a plain program's by a relative error of at most 0.014.
Values may be sent and summed in bfloat16 or wider, within the bound.
A program may use at most 64 MiB of HBM per device.

v0:
```python
import math

import jax
import jax.numpy as jnp
from jax import lax
from jax.sharding import PartitionSpec as P


def shifted(shard, axis, by):
    count = lax.axis_size(axis)
    pairs = [(i, i + by) for i in range(count) if 0 <= i + by < count]
    return lax.ppermute(shard, axis, pairs)


def angle_table(first, second, modulus):
    left = jnp.arange(first, dtype=jnp.int32)[:, None]
    right = jnp.arange(second, dtype=jnp.int32)[None, :]
    return (left * right % modulus).astype(jnp.float32) * (2.0 * math.pi / modulus)


def grid_sizes(length):
    total = 2 * length
    rows = math.gcd(total, 128)
    return (total, rows, total // rows)


def forward_dft(signal):
    count, length = signal.shape
    total, rows, cols = grid_sizes(length)
    half = rows // 2
    exact = lax.Precision.HIGH
    grid = signal.reshape(count, half, cols)
    first = angle_table(half, rows, rows)
    part_re = jnp.einsum("cab,ak->cbk", grid, jnp.cos(first), precision=exact)
    part_im = -jnp.einsum("cab,ak->cbk", grid, jnp.sin(first), precision=exact)
    twist = angle_table(cols, rows, total)
    twist_cos = jnp.cos(twist)
    twist_sin = jnp.sin(twist)
    turned_re = part_re * twist_cos + part_im * twist_sin
    turned_im = part_im * twist_cos - part_re * twist_sin
    second = angle_table(cols, cols, cols)
    second_cos = jnp.cos(second)
    second_sin = jnp.sin(second)
    out_re = jnp.einsum("cbk,bj->ckj", turned_re, second_cos, precision=exact) + jnp.einsum(
        "cbk,bj->ckj", turned_im, second_sin, precision=exact
    )
    out_im = jnp.einsum("cbk,bj->ckj", turned_im, second_cos, precision=exact) - jnp.einsum(
        "cbk,bj->ckj", turned_re, second_sin, precision=exact
    )
    return (out_re, out_im)


def inverse_dft(spec_re, spec_im, length):
    count = spec_re.shape[0]
    total, rows, cols = grid_sizes(length)
    half = rows // 2
    exact = lax.Precision.HIGH
    third = angle_table(cols, cols, cols)
    third_cos = jnp.cos(third)
    third_sin = jnp.sin(third)
    step_re = jnp.einsum("ckj,jb->ckb", spec_re, third_cos, precision=exact) - jnp.einsum(
        "ckj,jb->ckb", spec_im, third_sin, precision=exact
    )
    step_im = jnp.einsum("ckj,jb->ckb", spec_re, third_sin, precision=exact) + jnp.einsum(
        "ckj,jb->ckb", spec_im, third_cos, precision=exact
    )
    twist = angle_table(rows, cols, total)
    twist_cos = jnp.cos(twist)
    twist_sin = jnp.sin(twist)
    turned_re = step_re * twist_cos - step_im * twist_sin
    turned_im = step_re * twist_sin + step_im * twist_cos
    last = angle_table(rows, half, rows)
    result = jnp.einsum("ckb,ka->cab", turned_re, jnp.cos(last), precision=exact) - jnp.einsum(
        "ckb,ka->cab", turned_im, jnp.sin(last), precision=exact
    )
    return result.reshape(count, half * cols) / total


def long_filter(rates_local, residues_local, length):
    steps_axis = jnp.arange(length, dtype=jnp.float32)

    def add_mode(mode_index, total):
        rate_now = rates_local[mode_index][:, None]
        weight_now = residues_local[mode_index][:, None]
        return total + weight_now * jnp.sqrt(2.0 * rate_now) * jnp.exp(-rate_now * steps_axis)

    start = jnp.zeros((rates_local.shape[1], length), jnp.float32)
    return lax.fori_loop(0, rates_local.shape[0], add_mode, start)


def per_device(features, conv_weight, decay_rates, residues, skip_gain, out_weight):
    tok_rows = features.shape[1]
    width_local = features.shape[2]
    last_rows = features[:, tok_rows - 2 :, :]
    previous = shifted(last_rows, "ctx", 1)
    extended = jnp.concatenate([previous, features], axis=1).astype(jnp.float32)
    taps = conv_weight[:, :, :, None].transpose(0, 1, 3, 2)
    tp_start = lax.axis_index("tp") * width_local
    taps = lax.dynamic_slice_in_dim(taps, tp_start, width_local, 3)
    filtered = (
        taps[:, 0] * extended[:, 2:]
        + taps[:, 1] * extended[:, 1:-1]
        + taps[:, 2] * extended[:, :-2]
    )
    gate_in = (filtered[1] * filtered[2]).astype(jnp.bfloat16)
    by_channel = lax.all_to_all(gate_in.T, "ctx", split_axis=0, concat_axis=1, tiled=True)
    length = by_channel.shape[1]
    signal = by_channel.astype(jnp.float32)
    kernel = long_filter(decay_rates, residues, length)
    sig_re, sig_im = forward_dft(signal)
    ker_re, ker_im = forward_dft(kernel)
    prod_re = sig_re * ker_re - sig_im * ker_im
    prod_im = sig_re * ker_im + sig_im * ker_re
    convolved = inverse_dft(prod_re, prod_im, length)
    long_out = (convolved + skip_gain[:, None] * signal).astype(jnp.bfloat16)
    returned = lax.all_to_all(long_out, "ctx", split_axis=1, concat_axis=0, tiled=True)
    gated = (filtered[0] * returned.T.astype(jnp.float32)).astype(jnp.bfloat16)
    partial_sum = (
        jnp.dot(
            gated,
            lax.all_gather(out_weight, "ctx", axis=1, tiled=True),
            preferred_element_type=jnp.float32,
        )
        .astype(jnp.bfloat16)
        .astype(jnp.float32)
    )
    summed = lax.psum(partial_sum.astype(jnp.bfloat16), "tp").astype(jnp.float32)
    kept = lax.dynamic_slice_in_dim(summed, tp_start, width_local, 1)
    return kept.astype(jnp.bfloat16)


def solution(mesh):
    in_specs = (
        P(None, "ctx", "tp"),
        P(),
        P(None, ("tp", "ctx")),
        P(None, ("tp", "ctx")),
        P(("tp", "ctx")),
        P("tp", "ctx"),
    )
    out_specs = P("ctx", "tp")
    return jax.shard_map(
        per_device, mesh=mesh, in_specs=in_specs, out_specs=out_specs, check_vma=False
    )
```

profile of v0, /device:TPU:4, one launch (start us, length us, event | category | flops | bytes accessed | tf_op | source)
XLA Modules:
  0.0 274.4 jit_solution(14337545069532780381)
XLA Ops:
  7.3 1.4 slice.31
  8.7 1.9 collective-permute-start
  10.6 15.2 %while.14 = (s32[]{:T(128)}, f32[32,4096]{1,0:T(8,128)S(1)}, f32[16,32]{1,0:T(8,128)}, f32[16,32]{1,0:T(8,128)}, s32[]{:T(128)}, /*index=5*/s32[]{:T(128)}) while((s32[]{:T(128)}, f32[32,4096]{1,0:T(8,128)S(1)}, f32[16,32]{1,0:T(8,128)}, f32[16,32]{1,0:T(8,128)}, s32[]{:T(128)}, /*index=5*/s32[]{:T(128)}) %tuple.41), condition=%wide.region_1.0_spmd.clone, body=%wide.region_0.0_spmd.clone.sunk | while | flops 524387 | bytes 1049427 | solution.py:88
  27.1 1.0 convolution_negate_fusion.1
  28.1 1.0 fusion.56
  29.9 0.8 convolution_subtract_fusion.2
  31.2 2.3 copy.28
  33.5 1.3 copy.48
  34.8 2.0 copy.27
  36.8 2.0 maximum_convert_fusion
  38.8 2.4 fusion.5
  41.2 1.2 copy-done.1
  42.4 0.8 fusion.16
  43.1 12.4 %all-to-all-start = ((bf16[32,32,128]{2,1,0:T(8,128)(2,1)}), bf16[32,32,128]{2,1,0:T(8,128)(2,1)}, u32[]{:S(2)}, u32[]{:S(2)}) async-start(bf16[32,32,128]{2,1,0:T(8,128)(2,1)} %bitcast.90), calls=%async_computation | async-start | bytes 524288 | tf_op jit(solution)/shard_map/all_to_all | solution.py:106
  55.8 1.6 fusion.26
  57.4 0.8 fusion.102
  58.1 1.7 convolution_add_fusion.1
  59.9 8.3 %all-to-all-done = bf16[32,32,128]{2,1,0:T(8,128)(2,1)} async-done(((bf16[32,32,128]{2,1,0:T(8,128)(2,1)}), bf16[32,32,128]{2,1,0:T(8,128)(2,1)}, u32[]{:S(2)}, u32[]{:S(2)}) %all-to-all-start) | async-done | bytes 262176 | tf_op jit(solution)/shard_map/all_to_all | solution.py:106
  68.2 1.1 copy.29
  70.7 0.7 fusion.25
  71.5 0.7 fusion.24
  72.2 0.8 convolution_add_fusion.2
  73.5 1.1 multiply_add_fusion
  77.5 1.7 fusion.12
  79.2 1.7 fusion.8
  81.6 1.5 fusion.19
  83.1 20.5 %all_to_all.26 = bf16[32,32,128]{2,0,1:T(8,128)(2,1)S(1)} all-to-all(bf16[32,32,128]{2,0,1:T(8,128)(2,1)S(1)} %fusion.19), channel_id=1, replica_groups=mesh['ctx'=32,'tp'=8] {'ctx'}, dimensions={1} | all-to-all | bytes 524288 | tf_op jit(solution)/shard_map/all_to_all | solution.py:116
  103.6 1.1 fusion.18
  104.7 66.7 %all-gather.2.cloned.1.call-done = bf16[1024,8192]{1,0:T(8,128)(2,1)} async-done(((bf16[1024,256]{1,0:T(8,128)(2,1)}), bf16[1024,8192]{1,0:T(8,128)(2,1)}) %all-gather.2.cloned.1.call-update) | async-done | bytes 16777232 | tf_op jit(solution)/shard_map/all_gather | solution.py:121
  171.4 9.6 %convolution_convert_fusion = bf16[128,8192]{1,0:T(8,128)(2,1)} fusion(bf16[128,1024]{0,1:T(8,128)(2,1)S(1)} %fusion.18, bf16[1024,8192]{1,0:T(8,128)(2,1)} %all-gather.2.cloned.1.call-done), kind=kOutput, calls=%fused_computation.8 | convolution fusion | flops 2148532224 | bytes 19136512 | tf_op jit(solution)/shard_map/dot_general | solution.py:119
  181.0 84.9 %all-reduce.2.cloned.1.call-done = bf16[128,8192]{1,0:T(8,128)(2,1)} async-done(((bf16[128,8192]{1,0:T(8,128)(2,1)}), bf16[128,8192]{1,0:T(8,128)(2,1)}) %all-reduce.2.cloned.1.call-update) | async-done | bytes 2097168 | tf_op jit(solution)/shard_map/psum | solution.py:127
  265.9 1.7 convert_convert_fusion
  (79 shorter events, 23.8 us)
Async XLA Ops:
  6.5 19.7 %copy-start = (f32[3,3,8192]{2,1,0:T(4,128)S(1)}, f32[3,3,8192]{2,1,0:T(4,128)}, u32[]{:S(2)}) copy-start(f32[3,3,8192]{2,1,0:T(4,128)} %param.9) | copy-start | bytes 884740
  6.5 164.9 %all-gather.2.cloned.1.call-start = ((), (), s32[]{:S(2)}) async-start(), calls=%async_computation.2 | async-start | bytes 17301504 | tf_op jit(solution)/shard_map/all_gather | solution.py:121
  8.7 26.2 %collective-permute-start = (bf16[3,2,1024]{2,1,0:T(2,128)(2,1)}, bf16[3,2,1024]{2,1,0:T(2,128)(2,1)}, u32[]{:S(2)}, u32[]{:S(2)}) collective-permute-start(bf16[3,2,1024]{2,1,0:T(2,128)(2,1)} %slice.31), channel_id=1, source_target_pairs={{0,8},{8,16},{16,24},{24,32},{32,40},{40,48},{48,56},{56,64},{64,7... | collective-permute-start | bytes 36872 | tf_op jit(solution)/shard_map/ppermute | solution.py:12
  26.4 3.4 %copy-start.6 = (f32[64,128]{1,0:T(8,128)}, f32[64,128]{1,0:T(8,128)S(1)}, u32[]{:S(2)}) copy-start(f32[64,128]{1,0:T(8,128)S(1)} %get-tuple-element.135) | copy-start | bytes 98308
  26.4 4.2 %copy-start.3 = (f32[64,128]{1,0:T(8,128)}, f32[64,128]{1,0:T(8,128)S(1)}, u32[]{:S(2)}) copy-start(f32[64,128]{1,0:T(8,128)S(1)} %get-tuple-element.134) | copy-start | bytes 98308
  36.8 2.0 copy-start.11
  36.8 2.0 copy-start.12
  41.2 1.2 copy-start.1
  43.1 25.0 %all-to-all-start = ((bf16[32,32,128]{2,1,0:T(8,128)(2,1)}), bf16[32,32,128]{2,1,0:T(8,128)(2,1)}, u32[]{:S(2)}, u32[]{:S(2)}) async-start(bf16[32,32,128]{2,1,0:T(8,128)(2,1)} %bitcast.90), calls=%async_computation | async-start | bytes 524288 | tf_op jit(solution)/shard_map/all_to_all | solution.py:106
  55.5 210.4 %all-reduce.2.cloned.1.call-start = ((), (), s32[]{:S(2)}) async-start(), calls=%async_computation.3 | async-start | bytes 4194304 | tf_op jit(solution)/shard_map/psum | solution.py:127
  55.8 2.4 copy-start.4
  55.8 2.4 copy-start.7
  69.5 1.2 copy-start.5
  69.5 1.2 copy-start.8
  72.2 1.2 copy-start.2
  76.7 0.8 copy-start.9
  76.7 0.8 copy-start.10
  80.9 0.7 copy-start.13
Sparse Core Ops, SparseCore 0:
  9.9 161.4 all-gather.1
  181.1 84.7 all-reduce.1
where the time goes:
time: 276 us; the launch traced here: 274 us
  waiting for transfers between devices  161 us (58%)
  matrix products  27.2 us (10%)
  other arithmetic  25.1 us (9%)
  blocking collectives  20.5 us (7%)
  starting transfers between devices  14.5 us (5%)
  between operations  13.8 us (5%)
  local copies, waits for them, and re-layouts  12.3 us (4%)
    psum x1, waiting for transfers between devices, per_device(): lax.psum(partial_sum.astype(jnp.bfloat16), 'tp').astype(jnp.float32)  84.9 us
    all_gather x1, waiting for transfers between devices, per_device(): lax.all_gather(out_weight, 'ctx', axis=1, tiled=True)  66.7 us
    all_to_all x1, blocking collectives, per_device(): lax.all_to_all(long_out, 'ctx', split_axis=1, concat_axis=0, tiled=True)  20.5 us
    all_to_all x1, starting transfers between devices, per_device(): lax.all_to_all(gate_in.T, 'ctx', split_axis=0, concat_axis=1, tiled=True)  12.4 us
    mul x16, other arithmetic, add_mode(): weight_now * jnp.sqrt(2.0 * rate_now) * jnp.exp(-rate_now * steps_axis)  11.5 us
    dot_general x1, matrix products, per_device(): jnp.dot(gated, lax.all_gather(out_weight, 'ctx', axis=1, tiled=True), pre...  9.56 us
    all_to_all x1, waiting for transfers between devices, per_device(): lax.all_to_all(gate_in.T, 'ctx', split_axis=0, concat_axis=1, tiled=True)  8.31 us
    unnamed x31, local copies, waits for them, and re-layouts  6.34 us
  transfers between devices with their start and end apart: 4, of which 3 were waited for; matrix products, arithmetic and copies ran while one was open for 19% of the time, Pallas kernels for 0%

commit v1 on v0

v1 whole, which is shorter than its diff:
```python
import functools

import jax
import jax.numpy as jnp
from jax import lax
from jax.experimental import pallas as pl
from jax.experimental.pallas import tpu as pltpu
from jax.sharding import PartitionSpec as P

MESH = pl.DeviceIdType.MESH
F32 = jnp.float32
BF16 = jnp.bfloat16
LANES = 128
ROWS = 8
DECAY_STEPS = 6


def row_of(tile, index):
    return jnp.broadcast_to(tile[index : index + 1, :], (ROWS, LANES))


def kernel(
    dims,
    feats,
    conv_weight,
    pack,
    weight,
    out,
    params,
    halo,
    plain,
    gate_in,
    query,
    rates,
    gains,
    skips,
    decays,
    ends,
    ends_other,
    chip_end,
    chip_ends,
    carried,
    entry,
    entry_decay,
    gated_plain,
    gated,
    weights,
    part,
    parts,
    mixed,
    pieces,
    halo_sem,
    weight_sem,
    pair_sem,
    param_send,
    param_recv,
    chip_send,
    chip_recv,
    gated_send,
    gated_recv,
    part_send,
    part_recv,
    piece_send,
    piece_recv,
):
    nz, ny, n_ctx, n_tp = dims
    per_x = 2 * nz
    modes = rates.shape[1]
    tiles = feats.shape[2] // LANES
    half_tiles = tiles // 2
    steps = feats.shape[1] // ROWS
    width = feats.shape[2]
    me = lax.axis_index("ctx")
    tp = lax.axis_index("tp")
    core = lax.rem(me, 2)
    chip = lax.div(me, 2)
    x_hi = lax.div(me, per_x)
    z = lax.rem(chip, nz)
    x_lo = lax.div(tp, ny)
    y = lax.rem(tp, ny)
    own = lax.rem(me, per_x)
    partner = me + 1 - 2 * core
    x_partner = lax.rem(me + per_x, n_ctx)
    final_tp = x_lo * ny + lax.div(z, 2)
    final_base = x_hi * per_x + 4 * y

    def remote(src, dst, send, recv, device):
        return pltpu.make_async_remote_copy(
            src_ref=src, dst_ref=dst, send_sem=send, recv_sem=recv, device_id=device, device_id_type=MESH
        )

    barrier = pltpu.get_barrier_semaphore()

    def greet_ctx(step, carry):
        pl.semaphore_signal(barrier, inc=1, device_id={"ctx": lax.rem(me + step, n_ctx)}, device_id_type=MESH)
        return carry

    def greet_tp(step, carry):
        pl.semaphore_signal(barrier, inc=1, device_id={"tp": lax.rem(tp + step, n_tp)}, device_id_type=MESH)
        return carry

    lax.fori_loop(1, n_ctx, greet_ctx, 0)
    lax.fori_loop(1, n_tp, greet_tp, 0)
    apart = final_tp != tp

    @pl.when(apart)
    def _():
        for piece in range(4):
            pl.semaphore_signal(
                barrier, inc=1, device_id={"ctx": final_base + piece, "tp": final_tp}, device_id_type=MESH
            )

    params[me] = pack[...]
    weights[x_hi] = weight[...]

    pl.semaphore_wait(barrier, n_ctx + n_tp - 2 + jnp.where(apart, 4, 0))

    last_rows = pl.ds(feats.shape[1] - halo.shape[1], halo.shape[1])

    def halo_copy(device):
        return remote(feats.at[:, last_rows, :], halo, halo_sem.at[0], halo_sem.at[1], {"ctx": device})

    def param_copy(step, source, device):
        return remote(pack, params.at[source], param_send.at[step], param_recv.at[source], {"ctx": device})

    def weight_copy(slot):
        return remote(weight, weights.at[slot], weight_sem.at[0], weight_sem.at[1], {"ctx": x_partner})

    @pl.when(me < n_ctx - 1)
    def _():
        halo_copy(me + 1).start()

    def send_params(step, carry):
        param_copy(step, me, lax.rem(me + step, n_ctx)).start()
        return carry

    lax.fori_loop(1, n_ctx, send_params, 0)
    weight_copy(x_hi).start()

    @pl.when(me > 0)
    def _():
        halo_copy(me - 1).wait_recv()

    @pl.when(me == 0)
    def _():
        halo[...] = jnp.zeros_like(halo)

    row = lax.broadcasted_iota(jnp.int32, (ROWS, LANES), 0)
    lane_group = lax.broadcasted_iota(jnp.int32, (modes, LANES), 1) // (width // n_ctx)
    groups = LANES * n_ctx // width

    def short_conv(tile, carry):
        lanes = pl.ds(pl.multiple_of(tile * LANES, LANES), LANES)
        weight_lanes = pl.ds(pl.multiple_of(tp * width + tile * LANES, LANES), LANES)
        filtered = []
        for kind in range(3):
            plain[kind] = feats[kind, :, lanes].astype(F32)
            before = halo[kind, :, lanes].astype(F32)
            taps = conv_weight[kind, :, weight_lanes]
            tap = [row_of(taps, j) for j in range(3)]
            now = [plain[kind, pl.ds(step, ROWS, stride=steps), :] for step in range(steps)]
            last = halo.shape[1] - 1
            one = jnp.where(row == 0, row_of(before, last), pltpu.roll(now[steps - 1], 1, 0))
            two = jnp.where(row == 0, row_of(before, last - 1), pltpu.roll(now[steps - 2], 1, 0))
            chain = [two, one] + now
            filtered.append(
                [tap[0] * chain[s + 2] + tap[1] * chain[s + 1] + tap[2] * chain[s] for s in range(steps)]
            )
        for step in range(steps):
            query[tile, step] = filtered[0][step]
            gate_in[tile, step] = (filtered[1][step] * filtered[2][step]).astype(BF16).astype(F32)
        return carry

    lax.fori_loop(0, tiles, short_conv, 0)

    def wait_params(step, carry):
        source = lax.rem(me + step, n_ctx)
        param_copy(step, source, source).wait_recv()
        return carry

    lax.fori_loop(1, n_ctx, wait_params, 0)

    span = width // n_ctx

    def local_states(tile, carry):
        rate = jnp.zeros((modes, LANES), F32)
        residue = jnp.zeros((modes, LANES), F32)
        skip = jnp.zeros((modes, LANES), F32)
        for group in range(groups):
            piece = params[tile * groups + group]
            at = lambda which: pltpu.roll(piece, (group - which) * span % LANES, 1)
            mine = lane_group == group
            rate = jnp.where(mine, at(0), rate)
            residue = jnp.where(mine, at(1), residue)
            skip = jnp.where(mine, at(2), skip)
        rates[tile] = rate
        gains[tile] = residue * jnp.sqrt(2.0 * rate)
        skips[tile] = skip
        power = []
        for slot, tokens in enumerate((1, steps, 2 * steps, 4 * steps, 8 * steps, 16 * steps)):
            value = jnp.exp(-float(tokens) * rate)
            power.append(value)
            decays[slot, tile] = value
        signal = [gate_in[tile, step] for step in range(steps)]
        row_tokens = row.astype(F32) * float(steps)
        for mode in range(modes):
            decay = row_of(power[0], mode)
            state = signal[0]
            for step in range(1, steps):
                state = decay * state + signal[step]
            for slot in range(3):
                reach = 1 << slot
                factor = jnp.where(row >= reach, row_of(power[1 + slot], mode), 0.0)
                state = state + factor * pltpu.roll(state, reach, 0)
            ends[tile, mode : mode + 1, :] = state[ROWS - 1 :, :]
            entry[tile, mode] = jnp.where(row >= 1, pltpu.roll(state, 1, 0), 0.0)
            entry_decay[tile, mode] = jnp.exp(-row_tokens * row_of(rate, mode))
        return carry

    lax.fori_loop(0, tiles, local_states, 0)

    pair = remote(ends, ends_other, pair_sem.at[0], pair_sem.at[1], {"ctx": partner})
    pair.start()
    pair.wait_recv()
    half = pl.ds(core * half_tiles, half_tiles)
    mine, other = ends[half], ends_other[half]
    first = jnp.where(core == 0, mine, other)
    second = jnp.where(core == 0, other, mine)
    chip_end[...] = decays[4, half] * first + second
    n_chips = n_ctx // 2

    def chip_copy(source, target):
        return remote(
            chip_end, chip_ends.at[source], chip_send.at[target], chip_recv.at[source], {"ctx": 2 * target + core}
        )

    def send_chip(target, carry):
        chip_copy(chip, target).start()
        return carry

    lax.fori_loop(chip + 1, n_chips, send_chip, 0)
    long_decay = decays[5, half]

    def take_chip(source, total):
        chip_copy(source, source).wait_recv()
        return total * long_decay + chip_ends[source]

    carried[half] = lax.fori_loop(0, chip, take_chip, jnp.zeros(chip_end.shape, F32))
    give = remote(carried.at[half], carried.at[half], pair_sem.at[2], pair_sem.at[3], {"ctx": partner})
    give.start()
    other_half = pl.ds((1 - core) * half_tiles, half_tiles)
    remote(carried.at[half], carried.at[other_half], pair_sem.at[2], pair_sem.at[3], {"ctx": partner}).wait_recv()

    def long_conv(tile, carry):
        into_chip = carried[tile]
        into = jnp.where(core == 0, into_chip, decays[4, tile] * into_chip + ends_other[tile])
        power, gain = decays[0, tile], gains[tile]
        decay = [row_of(power, m) for m in range(modes)]
        weigh = [row_of(gain, m) for m in range(modes)]
        skip = row_of(skips[tile], 0)
        state = [entry[tile, m] + entry_decay[tile, m] * row_of(into, m) for m in range(modes)]
        for step in range(steps):
            signal = gate_in[tile, step]
            total = skip * signal
            for m in range(modes):
                state[m] = decay[m] * state[m] + signal
                total = total + weigh[m] * state[m]
            long_out = total.astype(BF16).astype(F32)
            gated_plain[pl.ds(step, ROWS, stride=steps), :] = query[tile, step] * long_out
        lanes = pl.ds(pl.multiple_of(tile * LANES, LANES), LANES)
        gated[own, :, lanes] = gated_plain[...].astype(BF16)
        return carry

    lax.fori_loop(0, tiles, long_conv, 0)

    def ring_device(to_z):
        return {"ctx": x_hi * per_x + 2 * to_z + core}

    def gated_copy(block, kind, step, device):
        return remote(
            gated.at[block], gated.at[block], gated_send.at[kind, step], gated_recv.at[block], device
        )

    up = ring_device(lax.rem(z + 1, nz))
    down = ring_device(lax.rem(z + nz - 1, nz))
    across = {"ctx": partner}
    up_steps, down_steps = nz // 2, nz - 1 - nz // 2

    def part_copy(source, block, side, device):
        slot = lax.rem(block, 4)
        return remote(
            part.at[block, side],
            parts.at[source, slot],
            part_send.at[block, side],
            part_recv.at[source, slot],
            {"tp": device},
        )

    def multiply(block):
        for side in range(2):
            value = jnp.dot(gated[block], weights[side], preferred_element_type=F32).astype(BF16)
            target = side * ny + lax.div(block, 4)

            @pl.when(target == tp)
            def _():
                parts[tp, lax.rem(block, 4)] = value

            @pl.when(target != tp)
            def _():
                part[block, side] = value
                part_copy(tp, block, side, target).start()

    gated_copy(own, 0, 0, up).start()
    gated_copy(own, 1, 0, down).start()
    gated_copy(own, 2, 0, across).start()
    weight_copy(1 - x_hi).wait_recv()
    multiply(own)
    for step in range(1, up_steps + 1):
        from_down = 2 * lax.rem(z + nz - step, nz) + core
        from_up = 2 * lax.rem(z + step, nz) + core
        gated_copy(from_down, 0, 0, up).wait_recv()
        if step < up_steps:
            gated_copy(from_down, 0, step, up).start()
        gated_copy(from_down, 2, step, across).start()
        if step <= down_steps:
            gated_copy(from_up, 1, 0, down).wait_recv()
            if step < down_steps:
                gated_copy(from_up, 1, step, down).start()
            gated_copy(from_up, 3, step, across).start()
        before = step - 1
        before_down = 2 * lax.rem(z + nz - before, nz) + 1 - core
        gated_copy(before_down, 2, 0, across).wait_recv()
        multiply(before_down)
        if 0 < before <= down_steps:
            before_up = 2 * lax.rem(z + before, nz) + 1 - core
            gated_copy(before_up, 2, 0, across).wait_recv()
            multiply(before_up)
        multiply(from_down)
        if step <= down_steps:
            multiply(from_up)
    last_down = 2 * lax.rem(z + nz - up_steps, nz) + 1 - core
    gated_copy(last_down, 2, 0, across).wait_recv()
    multiply(last_down)
    if up_steps <= down_steps:
        last_up = 2 * lax.rem(z + up_steps, nz) + 1 - core
        gated_copy(last_up, 2, 0, across).wait_recv()
        multiply(last_up)

    quarter = lax.rem(me, 4)

    def piece_copy(piece, slot):
        return remote(
            mixed.at[piece],
            pieces.at[slot],
            piece_send.at[piece],
            piece_recv.at[slot],
            {"ctx": final_base + piece, "tp": final_tp},
        )

    for piece in range(4):

        def take_part(step, total):
            source = lax.rem(tp + step, n_tp)
            remote(
                part.at[0, 0], parts.at[source, piece], part_send.at[0, 0], part_recv.at[source, piece], {"tp": source}
            ).wait_recv()
            return total + parts[source, piece].astype(F32)

        value = lax.fori_loop(1, n_tp, take_part, parts[tp, piece].astype(F32)).astype(BF16)
        here = jnp.logical_and(final_base + piece == me, final_tp == tp)

        @pl.when(here)
        def _():
            pieces[quarter] = value

        @pl.when(jnp.logical_not(here))
        def _():
            mixed[piece] = value
            piece_copy(piece, quarter).start()

    cols = out.shape[1] // 4
    for piece in range(4):
        here = jnp.logical_and(final_base + piece == me, final_tp == tp)

        @pl.when(jnp.logical_not(here))
        def _():
            piece_copy(piece, piece).wait_recv()

        out[:, piece * cols : (piece + 1) * cols] = pieces[piece]

    @pl.when(me < n_ctx - 1)
    def _():
        halo_copy(me + 1).wait_send()

    def drain_params(step, carry):
        param_copy(step, me, lax.rem(me + step, n_ctx)).wait_send()
        return carry

    lax.fori_loop(1, n_ctx, drain_params, 0)
    weight_copy(x_hi).wait_send()
    pair.wait_send()
    give.wait_send()

    def drain_chip(target, carry):
        chip_copy(chip, target).wait_send()
        return carry

    lax.fori_loop(chip + 1, n_chips, drain_chip, 0)
    for step in range(up_steps):
        gated_copy(own, 0, step, up).wait_send()
    for step in range(down_steps):
        gated_copy(own, 1, step, down).wait_send()
    for step in range(up_steps + 1):
        gated_copy(own, 2, step, across).wait_send()
    for step in range(1, down_steps + 1):
        gated_copy(own, 3, step, across).wait_send()

    def drain_parts(block, carry):
        for side in range(2):
            target = side * ny + lax.div(block, 4)

            @pl.when(target != tp)
            def _():
                part_copy(tp, block, side, target).wait_send()

        return carry

    lax.fori_loop(0, per_x, drain_parts, 0)
    for piece in range(4):
        here = jnp.logical_and(final_base + piece == me, final_tp == tp)

        @pl.when(jnp.logical_not(here))
        def _():
            piece_copy(piece, quarter).wait_send()


def per_device(n_ctx, n_tp, features, conv_weight, decay_rates, residues, skip_gain, out_weight):
    nz, ny = n_ctx // 4, n_tp // 2
    _, rows, width = features.shape
    modes, span = decay_rates.shape
    skip = jnp.broadcast_to(skip_gain[None, :], (modes, span))
    fill = jnp.zeros((modes, LANES - 3 * span), F32)
    pack = jnp.concatenate([decay_rates, residues, skip, fill], axis=1)
    tiles, steps = width // LANES, rows // ROWS
    cols = out_weight.shape[1]
    blocks = 2 * nz
    tile_state = (tiles, modes, LANES)
    row_state = (tiles, modes, ROWS, LANES)
    half_state = (tiles // 2, modes, LANES)
    dma = pltpu.SemaphoreType.DMA
    vmem = pl.BlockSpec(memory_space=pltpu.VMEM)
    return pl.pallas_call(
        functools.partial(kernel, (nz, ny, n_ctx, n_tp)),
        out_shape=jax.ShapeDtypeStruct((rows, 4 * cols), BF16),
        in_specs=[vmem] * 4,
        out_specs=vmem,
        scratch_shapes=[
            pltpu.VMEM((n_ctx, modes, LANES), F32),
            pltpu.VMEM((3, 16, width), BF16),
            pltpu.VMEM((3, rows, LANES), F32),
            pltpu.VMEM((tiles, steps, ROWS, LANES), F32),
            pltpu.VMEM((tiles, steps, ROWS, LANES), F32),
            pltpu.VMEM(tile_state, F32),
            pltpu.VMEM(tile_state, F32),
            pltpu.VMEM(tile_state, F32),
            pltpu.VMEM((DECAY_STEPS,) + tile_state, F32),
            pltpu.VMEM(tile_state, F32),
            pltpu.VMEM(tile_state, F32),
            pltpu.VMEM(half_state, F32),
            pltpu.VMEM((n_ctx // 2,) + half_state, F32),
            pltpu.VMEM(tile_state, F32),
            pltpu.VMEM(row_state, F32),
            pltpu.VMEM(row_state, F32),
            pltpu.VMEM((rows, LANES), F32),
            pltpu.VMEM((blocks, rows, width), BF16),
            pltpu.VMEM((2, width, cols), BF16),
            pltpu.VMEM((blocks, 2, rows, cols), BF16),
            pltpu.VMEM((n_tp, 4, rows, cols), BF16),
            pltpu.VMEM((4, rows, cols), BF16),
            pltpu.VMEM((4, rows, cols), BF16),
            dma((2,)),
            dma((2,)),
            dma((4,)),
            dma((n_ctx,)),
            dma((n_ctx,)),
            dma((n_ctx // 2,)),
            dma((n_ctx // 2,)),
            dma((4, nz)),
            dma((blocks,)),
            dma((blocks, 2)),
            dma((n_tp, 4)),
            dma((4,)),
            dma((4,)),
        ],
        compiler_params=pltpu.CompilerParams(
            collective_id=0, has_side_effects=True, vmem_limit_bytes=48 * 1024 * 1024
        ),
    )(features, conv_weight, pack, out_weight)


def solution(mesh):
    in_specs = (
        P(None, "ctx", "tp"),
        P(),
        P(None, ("tp", "ctx")),
        P(None, ("tp", "ctx")),
        P(("tp", "ctx")),
        P("tp", "ctx"),
    )
    return jax.shard_map(
        functools.partial(per_device, mesh.shape["ctx"], mesh.shape["tp"]),
        mesh=mesh,
        in_specs=in_specs,
        out_specs=P("ctx", "tp"),
        check_vma=False,
    )
```

time: 276 us -> 110 us (0.40)
  the two profiles are of different devices: /device:TPU:4 before, /device:TPU:21 now
where the time goes in v1:
time: 110 us
  Pallas kernels  104 us (95%)
  local copies, waits for them, and re-layouts  4.68 us (4%)
    pallas_call x1, Pallas kernels, per_device(): pl.pallas_call(functools.partial(kernel, (nz, ny, n_ctx, n_tp)), out_shap...  104 us
    unnamed x7, local copies, waits for them, and re-layouts  3.88 us

profile of v1, /device:TPU:21, one launch (start us, length us, event | category | flops | bytes accessed | tf_op | source)
XLA Modules:
  0.0 109.5 jit_solution(5442843358236667554)
XLA Ops:
  0.0 0.7 pad.2.clone
  0.7 0.1 pad.3.clone
  0.8 0.8 maximum_maximum_fusion.pack
  1.6 0.0 copy-start
  1.6 1.1 %copy-done = bf16[3,128,1024]{2,1,0:T(8,128)(2,1)S(1)} copy-done((bf16[3,128,1024]{2,1,0:T(8,128)(2,1)S(1)}, bf16[3,128,1024]{2,1,0:T(8,128)(2,1)}, u32[]{:S(2)}) %copy-start) | copy-done | bytes 786456
  2.7 0.0 copy-start.1
  2.7 1.0 copy-done.1
  3.8 0.0 copy-start.2
  3.8 1.0 copy-done.2
  4.8 104.0 %shard_map.64 = bf16[128,1024]{1,0:T(8,128)(2,1)S(1)} custom-call(bf16[3,128,1024]{2,1,0:T(8,128)(2,1)S(1)} %copy-done, f32[3,3,8192]{2,1,0:T(4,128)S(1)} %copy-done.2, f32[16,128]{1,0:T(8,128)S(1)} %maximum_maximum_fusion.pack, bf16[1024,256]{1,0:T(8,128)(2,1)S(1)} %copy-done.1), custom_call_target="tpu_custom_call" | custom-call | tf_op jit(solution)/shard_map/pallas_call | solution.py:452
  108.8 0.7 copy.8
  (1 shorter events, 0.0 us)
Async XLA Ops:
  1.6 1.1 %copy-start = (bf16[3,128,1024]{2,1,0:T(8,128)(2,1)S(1)}, bf16[3,128,1024]{2,1,0:T(8,128)(2,1)}, u32[]{:S(2)}) copy-start(bf16[3,128,1024]{2,1,0:T(8,128)(2,1)} %feats.1) | copy-start | bytes 2359300
  2.7 1.0 copy-start.1
  3.8 1.0 copy-start.2

commit v2 on v1

--- a/solution.py
+++ b/solution.py
@@ -12,6 +12,8 @@
 BF16 = jnp.bfloat16
 LANES = 128
 ROWS = 8
+CROSS_LAG = 3
+STRIP_LAG = 6
 DECAY_STEPS = 6
 
 
@@ -45,8 +47,11 @@
     gated_plain,
     gated,
     weights,
-    part,
-    parts,
+    kept,
+    crossing,
+    crossed,
+    summed,
+    strips,
     mixed,
     pieces,
     halo_sem,
@@ -56,10 +61,13 @@
     param_recv,
     chip_send,
     chip_recv,
-    gated_send,
+    ring_send,
+    across_send,
     gated_recv,
-    part_send,
-    part_recv,
+    cross_send,
+    cross_recv,
+    strip_send,
+    strip_recv,
     piece_send,
     piece_recv,
 ):
@@ -81,8 +89,9 @@
     own = lax.rem(me, per_x)
     partner = me + 1 - 2 * core
     x_partner = lax.rem(me + per_x, n_ctx)
-    final_tp = x_lo * ny + lax.div(z, 2)
-    final_base = x_hi * per_x + 4 * y
+    final_y = lax.div(z, 2)
+    quarter = lax.rem(me, 4)
+    strip_rows = feats.shape[1] // ny
 
     def remote(src, dst, send, recv, device):
         return pltpu.make_async_remote_copy(
@@ -101,19 +110,19 @@
 
     lax.fori_loop(1, n_ctx, greet_ctx, 0)
     lax.fori_loop(1, n_tp, greet_tp, 0)
-    apart = final_tp != tp
-
-    @pl.when(apart)
-    def _():
-        for piece in range(4):
+    for other_y in range(1, ny):
+        for which in range(4):
             pl.semaphore_signal(
-                barrier, inc=1, device_id={"ctx": final_base + piece, "tp": final_tp}, device_id_type=MESH
+                barrier,
+                inc=1,
+                device_id={"ctx": x_hi * per_x + 4 * y + which, "tp": x_lo * ny + lax.rem(y + other_y, ny)},
+                device_id_type=MESH,
             )
 
     params[me] = pack[...]
     weights[x_hi] = weight[...]
 
-    pl.semaphore_wait(barrier, n_ctx + n_tp - 2 + jnp.where(apart, 4, 0))
+    pl.semaphore_wait(barrier, n_ctx + n_tp - 2 + jnp.where(final_y != y, per_x, 0))
 
     last_rows = pl.ds(feats.shape[1] - halo.shape[1], halo.shape[1])
 
@@ -276,117 +285,154 @@
     def ring_device(to_z):
         return {"ctx": x_hi * per_x + 2 * to_z + core}
 
-    def gated_copy(block, kind, step, device):
+    devices = [ring_device(lax.rem(z + 1, nz)), ring_device(lax.rem(z + nz - 1, nz))]
+    far = nz // 2
+    half_rows = feats.shape[1] // 2
+
+    def ring_halves(way, step):
+        return [way, 1 - way] if step < far else [way]
+
+    def ring_block(way, step):
+        return 2 * lax.rem(z + (nz - step if way == 0 else step), nz) + core
+
+    def ring_copy(block, way, step, part):
+        rows = pl.ds(part * half_rows, half_rows)
         return remote(
-            gated.at[block], gated.at[block], gated_send.at[kind, step], gated_recv.at[block], device
-        )
-
-    up = ring_device(lax.rem(z + 1, nz))
-    down = ring_device(lax.rem(z + nz - 1, nz))
-    across = {"ctx": partner}
-    up_steps, down_steps = nz // 2, nz - 1 - nz // 2
-
-    def part_copy(source, block, side, device):
-        slot = lax.rem(block, 4)
+            gated.at[block, rows],
+            gated.at[block, rows],
+            ring_send.at[way, step, part],
+            gated_recv.at[block, part],
+            devices[way],
+        )
+
+    def across_copy(block, slot):
         return remote(
-            part.at[block, side],
-            parts.at[source, slot],
-            part_send.at[block, side],
-            part_recv.at[source, slot],
-            {"tp": device},
-        )
+            gated.at[block], gated.at[block], across_send.at[slot], gated_recv.at[block, 0], {"ctx": partner}
+        )
+
+    def cross_copy(block):
+        return remote(
+            crossing.at[block],
+            crossed.at[block],
+            cross_send.at[block],
+            cross_recv.at[block],
+            {"tp": (1 - x_lo) * ny + y},
+        )
+
+    def strip_copy(block, source, target):
+        rows = pl.ds(pl.multiple_of(target * strip_rows, strip_rows), strip_rows)
+        return remote(
+            summed.at[block, rows],
+            strips.at[source, block],
+            strip_send.at[block, target],
+            strip_recv.at[source, block],
+            {"tp": x_lo * ny + target},
+        )
+
+    def piece_copy(block, which, strip):
+        rows = pl.ds(pl.multiple_of(strip * strip_rows, strip_rows), strip_rows)
+        return remote(
+            mixed.at[block],
+            pieces.at[which, rows],
+            piece_send.at[block],
+            piece_recv.at[which, strip],
+            {"ctx": x_hi * per_x + block, "tp": x_lo * ny + final_y},
+        )
+
+    def stays(block):
+        return jnp.logical_and(block == own, final_y == y)
 
     def multiply(block):
-        for side in range(2):
-            value = jnp.dot(gated[block], weights[side], preferred_element_type=F32).astype(BF16)
-            target = side * ny + lax.div(block, 4)
-
-            @pl.when(target == tp)
+        value = jnp.dot(gated[block], weights[1 - x_lo], preferred_element_type=F32)
+        crossing[block] = value.astype(BF16)
+        cross_copy(block).start()
+        kept[block] = jnp.dot(gated[block], weights[x_lo], preferred_element_type=F32)
+
+    def combine(block):
+        cross_copy(block).wait_recv()
+        summed[block] = (kept[block] + crossed[block].astype(F32)).astype(BF16)
+        for step in range(1, ny):
+            strip_copy(block, y, lax.rem(y + step, ny)).start()
+
+    def finish(block):
+        own_rows = pl.ds(pl.multiple_of(y * strip_rows, strip_rows), strip_rows)
+        total = summed[block, own_rows].astype(F32)
+        for step in range(1, ny):
+            source = lax.rem(y + step, ny)
+            strip_copy(block, source, y).wait_recv()
+            total = total + strips[source, block].astype(F32)
+        value = total.astype(BF16)
+
+        @pl.when(stays(block))
+        def _():
+            pieces[quarter, own_rows] = value
+
+        @pl.when(jnp.logical_not(stays(block)))
+        def _():
+            mixed[block] = value
+            piece_copy(block, quarter, y).start()
+
+    for way in range(2):
+        for part in ring_halves(way, 1):
+            ring_copy(own, way, 0, part).start()
+    across_copy(own, 0).start()
+    weight_copy(1 - x_hi).wait_recv()
+
+    done = []
+
+    def advance(entry):
+        block, waits = entry
+        if waits:
+            across_copy(block, 0).wait_recv()
+        multiply(block)
+        done.append(block)
+        if len(done) > CROSS_LAG:
+            combine(done[-1 - CROSS_LAG])
+        if len(done) > STRIP_LAG:
+            finish(done[-1 - STRIP_LAG])
+
+    def other(block):
+        return block + 1 - 2 * core
+
+    pending = [(own, False)]
+    later = [(other(own), True)]
+    for step in range(1, far + 1):
+        ways = [0, 1]
+        arrived = [ring_block(way, step) for way in ways]
+        for turn in range(len(ring_halves(0, step))):
+            for way in ways:
+                part = ring_halves(way, step)[turn]
+                ring_copy(arrived[way], way, 0, part).wait_recv()
+                if step < far and part in ring_halves(way, step + 1):
+                    ring_copy(arrived[way], way, step, part).start()
+            if turn == 0:
+                for _ in range(min(2, len(pending))):
+                    advance(pending.pop(0))
+        blocks = arrived if step < far else arrived[:1]
+        for index, block in enumerate(blocks):
+            across_copy(block, 2 * step - 1 + index).start()
+        while pending:
+            advance(pending.pop(0))
+        pending = later + [(block, False) for block in blocks]
+        later = [(other(block), True) for block in blocks]
+    for entry_left in pending + later:
+        advance(entry_left)
+    total_blocks = len(done)
+    for index in range(total_blocks - CROSS_LAG, total_blocks):
+        combine(done[index])
+    for index in range(total_blocks - STRIP_LAG, total_blocks):
+        finish(done[index])
+
+    cols = out.shape[1] // 4
+    for which in range(4):
+        for strip in range(ny):
+            here = jnp.logical_and(jnp.logical_and(final_y == y, quarter == which), y == strip)
+
+            @pl.when(jnp.logical_not(here))
             def _():
-                parts[tp, lax.rem(block, 4)] = value
-
-            @pl.when(target != tp)
-            def _():
-                part[block, side] = value
-                part_copy(tp, block, side, target).start()
-
-    gated_copy(own, 0, 0, up).start()
-    gated_copy(own, 1, 0, down).start()
-    gated_copy(own, 2, 0, across).start()
-    weight_copy(1 - x_hi).wait_recv()
-    multiply(own)
-    for step in range(1, up_steps + 1):
-        from_down = 2 * lax.rem(z + nz - step, nz) + core
-        from_up = 2 * lax.rem(z + step, nz) + core
-        gated_copy(from_down, 0, 0, up).wait_recv()
-        if step < up_steps:
-            gated_copy(from_down, 0, step, up).start()
-        gated_copy(from_down, 2, step, across).start()
-        if step <= down_steps:
-            gated_copy(from_up, 1, 0, down).wait_recv()
-            if step < down_steps:
-                gated_copy(from_up, 1, step, down).start()
-            gated_copy(from_up, 3, step, across).start()
-        before = step - 1
-        before_down = 2 * lax.rem(z + nz - before, nz) + 1 - core
-        gated_copy(before_down, 2, 0, across).wait_recv()
-        multiply(before_down)
-        if 0 < before <= down_steps:
-            before_up = 2 * lax.rem(z + before, nz) + 1 - core
-            gated_copy(before_up, 2, 0, across).wait_recv()
-            multiply(before_up)
-        multiply(from_down)
-        if step <= down_steps:
-            multiply(from_up)
-    last_down = 2 * lax.rem(z + nz - up_steps, nz) + 1 - core
-    gated_copy(last_down, 2, 0, across).wait_recv()
-    multiply(last_down)
-    if up_steps <= down_steps:
-        last_up = 2 * lax.rem(z + up_steps, nz) + 1 - core
-        gated_copy(last_up, 2, 0, across).wait_recv()
-        multiply(last_up)
-
-    quarter = lax.rem(me, 4)
-
-    def piece_copy(piece, slot):
-        return remote(
-            mixed.at[piece],
-            pieces.at[slot],
-            piece_send.at[piece],
-            piece_recv.at[slot],
-            {"ctx": final_base + piece, "tp": final_tp},
-        )
-
-    for piece in range(4):
-
-        def take_part(step, total):
-            source = lax.rem(tp + step, n_tp)
-            remote(
-                part.at[0, 0], parts.at[source, piece], part_send.at[0, 0], part_recv.at[source, piece], {"tp": source}
-            ).wait_recv()
-            return total + parts[source, piece].astype(F32)
-
-        value = lax.fori_loop(1, n_tp, take_part, parts[tp, piece].astype(F32)).astype(BF16)
-        here = jnp.logical_and(final_base + piece == me, final_tp == tp)
-
-        @pl.when(here)
-        def _():
-            pieces[quarter] = value
-
-        @pl.when(jnp.logical_not(here))
-        def _():
-            mixed[piece] = value
-            piece_copy(piece, quarter).start()
-
-    cols = out.shape[1] // 4
-    for piece in range(4):
-        here = jnp.logical_and(final_base + piece == me, final_tp == tp)
-
-        @pl.when(jnp.logical_not(here))
-        def _():
-            piece_copy(piece, piece).wait_recv()
-
-        out[:, piece * cols : (piece + 1) * cols] = pieces[piece]
+                piece_copy(own, which, strip).wait_recv()
+
+        out[:, which * cols : (which + 1) * cols] = pieces[which]
 
     @pl.when(me < n_ctx - 1)
     def _():
@@ -406,32 +452,25 @@
         return carry
 
     lax.fori_loop(chip + 1, n_chips, drain_chip, 0)
-    for step in range(up_steps):
-        gated_copy(own, 0, step, up).wait_send()
-    for step in range(down_steps):
-        gated_copy(own, 1, step, down).wait_send()
-    for step in range(up_steps + 1):
-        gated_copy(own, 2, step, across).wait_send()
-    for step in range(1, down_steps + 1):
-        gated_copy(own, 3, step, across).wait_send()
-
-    def drain_parts(block, carry):
-        for side in range(2):
-            target = side * ny + lax.div(block, 4)
-
-            @pl.when(target != tp)
-            def _():
-                part_copy(tp, block, side, target).wait_send()
-
-        return carry
-
-    lax.fori_loop(0, per_x, drain_parts, 0)
-    for piece in range(4):
-        here = jnp.logical_and(final_base + piece == me, final_tp == tp)
-
-        @pl.when(jnp.logical_not(here))
+    for step in range(far):
+        for way in range(2):
+            for part in ring_halves(way, step + 1):
+                ring_copy(own, way, step, part).wait_send()
+    for slot in range(nz):
+        across_copy(own, slot).wait_send()
+
+    def drain_blocks(block, carry):
+        cross_copy(block).wait_send()
+        for step in range(1, ny):
+            strip_copy(block, y, lax.rem(y + step, ny)).wait_send()
+
+        @pl.when(jnp.logical_not(stays(block)))
         def _():
-            piece_copy(piece, quarter).wait_send()
+            piece_copy(block, quarter, y).wait_send()
+
+        return carry
+
+    lax.fori_loop(0, per_x, drain_blocks, 0)
 
 
 def per_device(n_ctx, n_tp, features, conv_weight, decay_rates, residues, skip_gain, out_weight):
@@ -474,9 +513,12 @@
             pltpu.VMEM((rows, LANES), F32),
             pltpu.VMEM((blocks, rows, width), BF16),
             pltpu.VMEM((2, width, cols), BF16),
-            pltpu.VMEM((blocks, 2, rows, cols), BF16),
-            pltpu.VMEM((n_tp, 4, rows, cols), BF16),
-            pltpu.VMEM((4, rows, cols), BF16),
+            pltpu.VMEM((blocks, rows, cols), F32),
+            pltpu.VMEM((blocks, rows, cols), BF16),
+            pltpu.VMEM((blocks, rows, cols), BF16),
+            pltpu.VMEM((blocks, rows, cols), BF16),
+            pltpu.VMEM((ny, blocks, rows // ny, cols), BF16),
+            pltpu.VMEM((blocks, rows // ny, cols), BF16),
             pltpu.VMEM((4, rows, cols), BF16),
             dma((2,)),
             dma((2,)),
@@ -485,12 +527,15 @@
             dma((n_ctx,)),
             dma((n_ctx // 2,)),
             dma((n_ctx // 2,)),
-            dma((4, nz)),
+            dma((2, nz // 2, 2)),
+            dma((nz,)),
+            dma((blocks, 2)),
             dma((blocks,)),
-            dma((blocks, 2)),
-            dma((n_tp, 4)),
-            dma((4,)),
-            dma((4,)),
+            dma((blocks,)),
+            dma((blocks, ny)),
+            dma((ny, blocks)),
+            dma((blocks,)),
+            dma((4, ny)),
         ],
         compiler_params=pltpu.CompilerParams(
             collective_id=0, has_side_effects=True, vmem_limit_bytes=48 * 1024 * 1024

time: 110 us -> 93.5 us (0.85)
  Pallas kernels: 104 us -> 87.8 us
    pallas_call x1, Pallas kernels: 104 us -> 87.8 us  [per_device(): pl.pallas_call(functools.partial(kernel, (nz, ny, n_ctx, n_tp)), out_shap...]
where the time goes in v2:
time: 93.5 us; the launch traced here: 93.3 us
  Pallas kernels  87.8 us (94%)
  local copies, waits for them, and re-layouts  4.68 us (5%)
    pallas_call x1, Pallas kernels, per_device(): pl.pallas_call(functools.partial(kernel, (nz, ny, n_ctx, n_tp)), out_shap...  87.8 us
    unnamed x7, local copies, waits for them, and re-layouts  3.88 us

profile of v2, /device:TPU:21, one launch (start us, length us, event | category | flops | bytes accessed | tf_op | source)
XLA Modules:
  0.0 93.3 jit_solution(8144442173789375594)
XLA Ops:
  0.0 0.7 pad.2.clone
  0.7 0.1 pad.3.clone
  0.8 0.8 maximum_maximum_fusion.pack
  1.6 0.0 copy-start
  1.6 1.1 %copy-done = bf16[3,128,1024]{2,1,0:T(8,128)(2,1)S(1)} copy-done((bf16[3,128,1024]{2,1,0:T(8,128)(2,1)S(1)}, bf16[3,128,1024]{2,1,0:T(8,128)(2,1)}, u32[]{:S(2)}) %copy-start) | copy-done | bytes 786456
  2.7 0.0 copy-start.1
  2.7 1.0 %copy-done.1 = bf16[1024,256]{1,0:T(8,128)(2,1)S(1)} copy-done((bf16[1024,256]{1,0:T(8,128)(2,1)S(1)}, bf16[1024,256]{1,0:T(8,128)(2,1)}, u32[]{:S(2)}) %copy-start.1) | copy-done | bytes 524312
  3.8 0.0 copy-start.2
  3.8 1.0 %copy-done.2 = f32[3,3,8192]{2,1,0:T(4,128)S(1)} copy-done((f32[3,3,8192]{2,1,0:T(4,128)S(1)}, f32[3,3,8192]{2,1,0:T(4,128)}, u32[]{:S(2)}) %copy-start.2) | copy-done | bytes 294936
  4.8 87.8 %shard_map.64 = bf16[128,1024]{1,0:T(8,128)(2,1)S(1)} custom-call(bf16[3,128,1024]{2,1,0:T(8,128)(2,1)S(1)} %copy-done, f32[3,3,8192]{2,1,0:T(4,128)S(1)} %copy-done.2, f32[16,128]{1,0:T(8,128)S(1)} %maximum_maximum_fusion.pack, bf16[1024,256]{1,0:T(8,128)(2,1)S(1)} %copy-done.1), custom_call_target="tpu_custom_call" | custom-call | tf_op jit(solution)/shard_map/pallas_call | solution.py:491
  92.6 0.7 copy.8
  (1 shorter events, 0.0 us)
Async XLA Ops:
  1.6 1.1 %copy-start = (bf16[3,128,1024]{2,1,0:T(8,128)(2,1)S(1)}, bf16[3,128,1024]{2,1,0:T(8,128)(2,1)}, u32[]{:S(2)}) copy-start(bf16[3,128,1024]{2,1,0:T(8,128)(2,1)} %feats.1) | copy-start | bytes 2359300
  2.7 1.0 %copy-start.1 = (bf16[1024,256]{1,0:T(8,128)(2,1)S(1)}, bf16[1024,256]{1,0:T(8,128)(2,1)}, u32[]{:S(2)}) copy-start(bf16[1024,256]{1,0:T(8,128)(2,1)} %weight.1) | copy-start | bytes 1572868
  3.8 1.0 %copy-start.2 = (f32[3,3,8192]{2,1,0:T(4,128)S(1)}, f32[3,3,8192]{2,1,0:T(4,128)}, u32[]{:S(2)}) copy-start(f32[3,3,8192]{2,1,0:T(4,128)} %conv_weight.1) | copy-start | bytes 884740

commit v3 on v2

--- a/solution.py
+++ b/solution.py
@@ -23,11 +23,19 @@
 
 def kernel(
     dims,
+    features,
+    all_taps,
+    decay_rates,
+    residues,
+    skip_gain,
+    weight,
+    out,
     feats,
     conv_weight,
+    own_rates,
+    own_residues,
+    own_skip,
     pack,
-    weight,
-    out,
     params,
     halo,
     plain,
@@ -54,6 +62,7 @@
     strips,
     mixed,
     pieces,
+    fetch_sem,
     halo_sem,
     weight_sem,
     pair_sem,
@@ -98,6 +107,23 @@
             src_ref=src, dst_ref=dst, send_sem=send, recv_sem=recv, device_id=device, device_id_type=MESH
         )
 
+    own_lanes = pl.ds(pl.multiple_of(tp * width, width), width)
+    fetches = [
+        pltpu.make_async_copy(src, dst, fetch_sem.at[slot])
+        for slot, (src, dst) in enumerate(
+            [
+                (decay_rates, own_rates),
+                (residues, own_residues),
+                (skip_gain, own_skip),
+                (features, feats),
+                (all_taps.at[:, :, own_lanes], conv_weight),
+                (weight, weights.at[x_hi]),
+            ]
+        )
+    ]
+    for fetch in fetches:
+        fetch.start()
+
     barrier = pltpu.get_barrier_semaphore()
 
     def greet_ctx(step, carry):
@@ -119,8 +145,20 @@
                 device_id_type=MESH,
             )
 
-    params[me] = pack[...]
-    weights[x_hi] = weight[...]
+    for fetch in fetches:
+        fetch.wait()
+    modes_shape = own_rates.shape
+    packed = jnp.concatenate(
+        [
+            own_rates[...],
+            own_residues[...],
+            jnp.broadcast_to(own_skip[...], modes_shape),
+            jnp.zeros((modes_shape[0], LANES - 3 * modes_shape[1]), F32),
+        ],
+        axis=1,
+    )
+    pack[...] = packed
+    params[me] = packed
 
     pl.semaphore_wait(barrier, n_ctx + n_tp - 2 + jnp.where(final_y != y, per_x, 0))
 
@@ -133,7 +171,7 @@
         return remote(pack, params.at[source], param_send.at[step], param_recv.at[source], {"ctx": device})
 
     def weight_copy(slot):
-        return remote(weight, weights.at[slot], weight_sem.at[0], weight_sem.at[1], {"ctx": x_partner})
+        return remote(weights.at[slot], weights.at[slot], weight_sem.at[0], weight_sem.at[1], {"ctx": x_partner})
 
     @pl.when(me < n_ctx - 1)
     def _():
@@ -144,7 +182,6 @@
         return carry
 
     lax.fori_loop(1, n_ctx, send_params, 0)
-    weight_copy(x_hi).start()
 
     @pl.when(me > 0)
     def _():
@@ -160,12 +197,11 @@
 
     def short_conv(tile, carry):
         lanes = pl.ds(pl.multiple_of(tile * LANES, LANES), LANES)
-        weight_lanes = pl.ds(pl.multiple_of(tp * width + tile * LANES, LANES), LANES)
         filtered = []
         for kind in range(3):
             plain[kind] = feats[kind, :, lanes].astype(F32)
             before = halo[kind, :, lanes].astype(F32)
-            taps = conv_weight[kind, :, weight_lanes]
+            taps = conv_weight[kind, :, lanes]
             tap = [row_of(taps, j) for j in range(3)]
             now = [plain[kind, pl.ds(step, ROWS, stride=steps), :] for step in range(steps)]
             last = halo.shape[1] - 1
@@ -188,6 +224,7 @@
         return carry
 
     lax.fori_loop(1, n_ctx, wait_params, 0)
+    weight_copy(x_hi).start()
 
     span = width // n_ctx
 
@@ -477,9 +514,6 @@
     nz, ny = n_ctx // 4, n_tp // 2
     _, rows, width = features.shape
     modes, span = decay_rates.shape
-    skip = jnp.broadcast_to(skip_gain[None, :], (modes, span))
-    fill = jnp.zeros((modes, LANES - 3 * span), F32)
-    pack = jnp.concatenate([decay_rates, residues, skip, fill], axis=1)
     tiles, steps = width // LANES, rows // ROWS
     cols = out_weight.shape[1]
     blocks = 2 * nz
@@ -491,9 +525,15 @@
     return pl.pallas_call(
         functools.partial(kernel, (nz, ny, n_ctx, n_tp)),
         out_shape=jax.ShapeDtypeStruct((rows, 4 * cols), BF16),
-        in_specs=[vmem] * 4,
+        in_specs=[pl.BlockSpec(memory_space=pltpu.HBM)] * 6,
         out_specs=vmem,
         scratch_shapes=[
+            pltpu.VMEM(features.shape, BF16),
+            pltpu.VMEM(conv_weight.shape[:2] + (width,), F32),
+            pltpu.VMEM((modes, span), F32),
+            pltpu.VMEM((modes, span), F32),
+            pltpu.VMEM((1, span), F32),
+            pltpu.VMEM((modes, LANES), F32),
             pltpu.VMEM((n_ctx, modes, LANES), F32),
             pltpu.VMEM((3, 16, width), BF16),
             pltpu.VMEM((3, rows, LANES), F32),
@@ -520,6 +560,7 @@
             pltpu.VMEM((ny, blocks, rows // ny, cols), BF16),
             pltpu.VMEM((blocks, rows // ny, cols), BF16),
             pltpu.VMEM((4, rows, cols), BF16),
+            dma((6,)),
             dma((2,)),
             dma((2,)),
             dma((4,)),
@@ -538,9 +579,9 @@
             dma((4, ny)),
         ],
         compiler_params=pltpu.CompilerParams(
-            collective_id=0, has_side_effects=True, vmem_limit_bytes=48 * 1024 * 1024
+            collective_id=0, has_side_effects=True, vmem_limit_bytes=67_000_000
         ),
-    )(features, conv_weight, pack, out_weight)
+    )(features, conv_weight, decay_rates, residues, skip_gain[None, :], out_weight)
 
 
 def solution(mesh):

time: 93.5 us -> 93.2 us (level)
  Pallas kernels: 87.8 us -> 91.1 us
  local copies, waits for them, and re-layouts: 4.68 us -> 1.67 us
    pallas_call x1, Pallas kernels: 87.8 us -> 91.1 us  [per_device(): pl.pallas_call(functools.partial(kernel, (nz, ny, n_ctx, n_tp)), out_shap...]
    unnamed x7 -> x1, local copies, waits for them, and re-layouts: 3.88 us -> 1.67 us
where the time goes in v3:
time: 93.2 us; the launch traced here: 92.8 us
  Pallas kernels  91.1 us (98%)
  local copies, waits for them, and re-layouts  1.67 us (2%)
    pallas_call x1, Pallas kernels, per_device(): pl.pallas_call(functools.partial(kernel, (nz, ny, n_ctx, n_tp)), out_shap...  91.1 us

profile of v3, /device:TPU:21, one launch (start us, length us, event | category | flops | bytes accessed | tf_op | source)
XLA Modules:
  0.0 92.8 jit_solution(18441686035234683432)
XLA Ops:
  0.0 91.1 %shard_map.64 = bf16[128,1024]{1,0:T(8,128)(2,1)} custom-call(bf16[3,128,1024]{2,1,0:T(8,128)(2,1)} %features.1, f32[3,3,8192]{2,1,0:T(4,128)} %all_taps.1, f32[16,32]{1,0:T(8,128)} %decay_rates.1, f32[16,32]{1,0:T(8,128)} %residues.1, f32[1,32]{1,0:T(1,128)} %bitcast.1, bf16[1024,256]{1,0:T(8,128)(2,1)} %weight.1), custom_call_target="tpu_custom_call" | custom-call | tf_op jit(solution)/shard_map/pallas_call | solution.py:525
  91.1 1.7 %copy.8 = bf16[128,1024]{1,0:T(8,128)(2,1)} copy(bf16[128,1024]{1,0:T(8,128)(2,1)} %shard_map.64) | data formatting | bytes 524288

commit v4 on v3

--- a/solution.py
+++ b/solution.py
@@ -49,6 +49,7 @@
     ends_other,
     chip_end,
     chip_ends,
+    plane_total,
     carried,
     entry,
     entry_decay,
@@ -70,6 +71,7 @@
     param_recv,
     chip_send,
     chip_recv,
+    plane_sem,
     ring_send,
     across_send,
     gated_recv,
@@ -177,11 +179,19 @@
     def _():
         halo_copy(me + 1).start()
 
+    n_chips = n_ctx // 2
+
+    def chip_at(step):
+        return 2 * lax.rem(chip + step, n_chips) + core
+
     def send_params(step, carry):
-        param_copy(step, me, lax.rem(me + step, n_ctx)).start()
-        return carry
-
-    lax.fori_loop(1, n_ctx, send_params, 0)
+        param_copy(step, me, chip_at(step)).start()
+        return carry
+
+    own_across = remote(pack, params.at[me], param_send.at[0], param_recv.at[me], {"ctx": partner})
+    own_across.start()
+    lax.fori_loop(1, n_chips, send_params, 0)
+    weight_copy(x_hi).start()
 
     @pl.when(me > 0)
     def _():
@@ -218,13 +228,28 @@
 
     lax.fori_loop(0, tiles, short_conv, 0)
 
+    def relay_copy(step, source):
+        return remote(
+            params.at[source],
+            params.at[source],
+            param_send.at[n_chips + step],
+            param_recv.at[source],
+            {"ctx": partner},
+        )
+
+    def relay_params(step, carry):
+        source = chip_at(step)
+        param_copy(step, source, source).wait_recv()
+        relay_copy(step, source).start()
+        return carry
+
+    lax.fori_loop(1, n_chips, relay_params, 0)
+
     def wait_params(step, carry):
-        source = lax.rem(me + step, n_ctx)
-        param_copy(step, source, source).wait_recv()
-        return carry
-
-    lax.fori_loop(1, n_ctx, wait_params, 0)
-    weight_copy(x_hi).start()
+        relay_copy(0, chip_at(step) + 1 - 2 * core).wait_recv()
+        return carry
+
+    lax.fori_loop(0, n_chips, wait_params, 0)
 
     span = width // n_ctx
 
@@ -273,27 +298,52 @@
     first = jnp.where(core == 0, mine, other)
     second = jnp.where(core == 0, other, mine)
     chip_end[...] = decays[4, half] * first + second
-    n_chips = n_ctx // 2
 
     def chip_copy(source, target):
         return remote(
             chip_end, chip_ends.at[source], chip_send.at[target], chip_recv.at[source], {"ctx": 2 * target + core}
         )
 
-    def send_chip(target, carry):
-        chip_copy(chip, target).start()
-        return carry
-
-    lax.fori_loop(chip + 1, n_chips, send_chip, 0)
+    def each_target(act):
+        def body(step, carry):
+            to_z = lax.rem(z + step, nz)
+
+            @pl.when(jnp.logical_or(x_hi == 0, to_z > z))
+            def _():
+                act(chip_copy(chip, x_hi * nz + to_z))
+
+            return carry
+
+        lax.fori_loop(1, nz, body, 0)
+
+    each_target(lambda copy: copy.start())
     long_decay = decays[5, half]
-
-    def take_chip(source, total):
+    total_copy = remote(plane_total, plane_total, plane_sem.at[0], plane_sem.at[1], {"ctx": x_partner})
+
+    def take_chip(source, state):
+        total, power = state
         chip_copy(source, source).wait_recv()
-        return total * long_decay + chip_ends[source]
-
-    carried[half] = lax.fori_loop(0, chip, take_chip, jnp.zeros(chip_end.shape, F32))
+        return total * long_decay + chip_ends[source], power * long_decay
+
+    nothing = jnp.zeros(chip_end.shape, F32)
+    before_here, reach_back = lax.fori_loop(x_hi * nz, chip, take_chip, (nothing, nothing + 1.0))
+    carried[half] = before_here
+
+    @pl.when(x_hi == 1)
+    def _():
+        total_copy.wait_recv()
+        carried[half] = carried[half] + reach_back * plane_total[...]
+
     give = remote(carried.at[half], carried.at[half], pair_sem.at[2], pair_sem.at[3], {"ctx": partner})
     give.start()
+
+    @pl.when(x_hi == 0)
+    def _():
+        through_here = before_here * long_decay + chip_end[...]
+        whole, _ = lax.fori_loop(chip + 1, nz, take_chip, (through_here, nothing))
+        plane_total[...] = whole
+        total_copy.start()
+
     other_half = pl.ds((1 - core) * half_tiles, half_tiles)
     remote(carried.at[half], carried.at[other_half], pair_sem.at[2], pair_sem.at[3], {"ctx": partner}).wait_recv()
 
@@ -476,19 +526,22 @@
         halo_copy(me + 1).wait_send()
 
     def drain_params(step, carry):
-        param_copy(step, me, lax.rem(me + step, n_ctx)).wait_send()
-        return carry
-
-    lax.fori_loop(1, n_ctx, drain_params, 0)
+        param_copy(step, me, chip_at(step)).wait_send()
+        relay_copy(step, chip_at(step)).wait_send()
+        return carry
+
+    own_across.wait_send()
+    lax.fori_loop(1, n_chips, drain_params, 0)
     weight_copy(x_hi).wait_send()
     pair.wait_send()
     give.wait_send()
 
-    def drain_chip(target, carry):
-        chip_copy(chip, target).wait_send()
-        return carry
-
-    lax.fori_loop(chip + 1, n_chips, drain_chip, 0)
+    each_target(lambda copy: copy.wait_send())
+
+    @pl.when(x_hi == 0)
+    def _():
+        total_copy.wait_send()
+
     for step in range(far):
         for way in range(2):
             for part in ring_halves(way, step + 1):
@@ -547,6 +600,7 @@
             pltpu.VMEM(tile_state, F32),
             pltpu.VMEM(half_state, F32),
             pltpu.VMEM((n_ctx // 2,) + half_state, F32),
+            pltpu.VMEM(half_state, F32),
             pltpu.VMEM(tile_state, F32),
             pltpu.VMEM(row_state, F32),
             pltpu.VMEM(row_state, F32),
@@ -568,6 +622,7 @@
             dma((n_ctx,)),
             dma((n_ctx // 2,)),
             dma((n_ctx // 2,)),
+            dma((2,)),
             dma((2, nz // 2, 2)),
             dma((nz,)),
             dma((blocks, 2)),

time: 93.2 us -> 86.1 us (0.924)
  Pallas kernels: 91.1 us -> 83.9 us
    pallas_call x1, Pallas kernels: 91.1 us -> 83.9 us  [per_device(): pl.pallas_call(functools.partial(kernel, (nz, ny, n_ctx, n_tp)), out_shap...]
where the time goes in v4:
time: 86.1 us; the launch traced here: 85.6 us
  Pallas kernels  83.9 us (97%)
  local copies, waits for them, and re-layouts  1.67 us (2%)
    pallas_call x1, Pallas kernels, per_device(): pl.pallas_call(functools.partial(kernel, (nz, ny, n_ctx, n_tp)), out_shap...  83.9 us

profile of v4, /device:TPU:21, one launch (start us, length us, event | category | flops | bytes accessed | tf_op | source)
XLA Modules:
  0.0 85.6 jit_solution(11663704890810079976)
XLA Ops:
  0.0 83.9 %shard_map.64 = bf16[128,1024]{1,0:T(8,128)(2,1)} custom-call(bf16[3,128,1024]{2,1,0:T(8,128)(2,1)} %features.1, f32[3,3,8192]{2,1,0:T(4,128)} %all_taps.1, f32[16,32]{1,0:T(8,128)} %decay_rates.1, f32[16,32]{1,0:T(8,128)} %residues.1, f32[1,32]{1,0:T(1,128)} %bitcast.1, bf16[1024,256]{1,0:T(8,128)(2,1)} %weight.1), custom_call_target="tpu_custom_call" | custom-call | tf_op jit(solution)/shard_map/pallas_call | solution.py:578
  83.9 1.7 %copy.8 = bf16[128,1024]{1,0:T(8,128)(2,1)} copy(bf16[128,1024]{1,0:T(8,128)(2,1)} %shard_map.64) | data formatting | bytes 524288

commit v5 on v4

--- a/solution.py
+++ b/solution.py
@@ -486,6 +486,10 @@
     for step in range(1, far + 1):
         ways = [0, 1]
         arrived = [ring_block(way, step) for way in ways]
+        if step == far:
+            for waiting in pending + later:
+                advance(waiting)
+            pending, later = [], []
         for turn in range(len(ring_halves(0, step))):
             for way in ways:
                 part = ring_halves(way, step)[turn]

time: 86.1 us -> 86.1 us (level)
  no operation moved by 1% of the time
where the time goes in v5:
time: 86.1 us; the launch traced here: 85.3 us
  Pallas kernels  83.7 us (97%)
  local copies, waits for them, and re-layouts  1.67 us (2%)
    pallas_call x1, Pallas kernels, per_device(): pl.pallas_call(functools.partial(kernel, (nz, ny, n_ctx, n_tp)), out_shap...  83.7 us

profile of v5, /device:TPU:21, one launch (start us, length us, event | category | flops | bytes accessed | tf_op | source)
XLA Modules:
  0.0 85.3 jit_solution(17965122471839271909)
XLA Ops:
  0.0 83.7 %shard_map.64 = bf16[128,1024]{1,0:T(8,128)(2,1)} custom-call(bf16[3,128,1024]{2,1,0:T(8,128)(2,1)} %features.1, f32[3,3,8192]{2,1,0:T(4,128)} %all_taps.1, f32[16,32]{1,0:T(8,128)} %decay_rates.1, f32[16,32]{1,0:T(8,128)} %residues.1, f32[1,32]{1,0:T(1,128)} %bitcast.1, bf16[1024,256]{1,0:T(8,128)(2,1)} %weight.1), custom_call_target="tpu_custom_call" | custom-call | tf_op jit(solution)/shard_map/pallas_call | solution.py:582
  83.7 1.7 %copy.8 = bf16[128,1024]{1,0:T(8,128)(2,1)} copy(bf16[128,1024]{1,0:T(8,128)(2,1)} %shard_map.64) | data formatting | bytes 524288

commit v6 on v5

--- a/solution.py
+++ b/solution.py
@@ -191,7 +191,6 @@
     own_across = remote(pack, params.at[me], param_send.at[0], param_recv.at[me], {"ctx": partner})
     own_across.start()
     lax.fori_loop(1, n_chips, send_params, 0)
-    weight_copy(x_hi).start()
 
     @pl.when(me > 0)
     def _():
@@ -317,6 +316,7 @@
         lax.fori_loop(1, nz, body, 0)
 
     each_target(lambda copy: copy.start())
+    weight_copy(x_hi).start()
     long_decay = decays[5, half]
     total_copy = remote(plane_total, plane_total, plane_sem.at[0], plane_sem.at[1], {"ctx": x_partner})
 

time: 86.1 us -> 88.7 us (1.030)
  Pallas kernels: 83.7 us -> 86.3 us
    pallas_call x1, Pallas kernels: 83.7 us -> 86.3 us  [per_device(): pl.pallas_call(functools.partial(kernel, (nz, ny, n_ctx, n_tp)), out_shap...]
where the time goes in v6:
time: 88.7 us; the launch traced here: 88 us
  Pallas kernels  86.3 us (97%)
  local copies, waits for them, and re-layouts  1.67 us (2%)
    pallas_call x1, Pallas kernels, per_device(): pl.pallas_call(functools.partial(kernel, (nz, ny, n_ctx, n_tp)), out_shap...  86.3 us

profile of v6, /device:TPU:21, one launch (start us, length us, event | category | flops | bytes accessed | tf_op | source)
XLA Modules:
  0.0 88.0 jit_solution(4062005793196190147)
XLA Ops:
  0.0 86.3 %shard_map.64 = bf16[128,1024]{1,0:T(8,128)(2,1)} custom-call(bf16[3,128,1024]{2,1,0:T(8,128)(2,1)} %features.1, f32[3,3,8192]{2,1,0:T(4,128)} %all_taps.1, f32[16,32]{1,0:T(8,128)} %decay_rates.1, f32[16,32]{1,0:T(8,128)} %residues.1, f32[1,32]{1,0:T(1,128)} %bitcast.1, bf16[1024,256]{1,0:T(8,128)(2,1)} %weight.1), custom_call_target="tpu_custom_call" | custom-call | tf_op jit(solution)/shard_map/pallas_call | solution.py:582
  86.3 1.7 %copy.8 = bf16[128,1024]{1,0:T(8,128)(2,1)} copy(bf16[128,1024]{1,0:T(8,128)(2,1)} %shard_map.64) | data formatting | bytes 524288
